TPU v7x, 32 devices: a whole 2x2x4 slice. The times are simulated.
32 devices in a mesh: row: 4 (over z), col: 8 (over y, x, core).
Axes of the slice: x: 2, y: 2, z: 4, core: 2. Of those that a mesh axis runs over, the one named last changes fastest.
Arguments:
- src_points: bfloat16 [512, 32, 256], P('row'), may hold values from -6 to 6
- tgt_points: bfloat16 [64, 32, 256], P('col'), may hold values from -6 to 6
- log_src: float32 [512, 256], P('row'), may hold values from -4 to 4
- log_tgt: float32 [64, 256], P('col'), may hold values from -4 to 4
- tgt_potential: float32 [64, 256], P('col'), may hold values from -1 to 25
- pattern: int32 [512, 4], P('row'), may hold values from 0 to 63, as said below
Outputs:
- src_new: float32 [512, 256], P('row')
- tgt_new: float32 [64, 256], P('col')
Inputs may be any that keep to these rules, and one draw needn't show every extreme that they name: `pattern`: each row names 4 different target blocks. For every index of row and every index of col, at most 128 of the entries in that index's source blocks name a target block held by that index of col, and exactly 128 do for some index of col. Every target block is named by some entry.
All inputs are finite; a program needn't handle non-finite values.
Results may differ from a plain program's by a relative error of at most 0.0015.
Values may be sent and summed in bfloat16 or wider, within the bound.
No kernel may reach another device: no remote copies, remote signals or barrier semaphores. Data moves between devices by JAX's collectives and lax.ppermute only.
A program may use at most 64 MiB of HBM per device.

v0:
```python
import math
import jax
import jax.numpy as jnp
from jax import lax
from jax.sharding import PartitionSpec as P

DIM = 32
FANOUT = 4
PAIR_MEAN = 64
epsilon = 0.1
very_low = -1e30
entry_batch = 8


def joined(value, axis, join):
    pieces = jax.tree.map(lambda part: lax.all_gather(part, axis), value)
    head = jax.tree.map(lambda part: part[0], pieces)
    tail = jax.tree.map(lambda part: part[1:], pieces)
    subtotal, _ = lax.scan(lambda subtotal, share: (join(subtotal, share), None), head, tail)
    return subtotal


def merge_parts(left_part, right_part):
    top_score = jnp.maximum(left_part[0], right_part[0])
    exp_total = left_part[1] * jnp.exp(left_part[0] - top_score) + right_part[1] * jnp.exp(
        right_part[0] - top_score
    )
    return (top_score, exp_total)


def pick_rows(table, row_ids, precise):
    table_rows = table.shape[0]
    flat = table.reshape(table_rows, -1)
    selector = (row_ids[:, None] == jnp.arange(table_rows, dtype=jnp.int32)[None, :]).astype(
        flat.dtype
    )
    if precise:
        picked = jnp.dot(
            selector, flat, precision=lax.Precision.HIGHEST, preferred_element_type=jnp.float32
        )
    else:
        picked = jnp.dot(selector, flat, preferred_element_type=jnp.float32).astype(table.dtype)
    return picked.reshape((row_ids.shape[0],) + table.shape[1:])


def collect_rows(row_total_count, row_ids, part_top, part_total):
    group = math.gcd(row_total_count, 32)

    def group_top(first_row):
        group_ids = first_row + jnp.arange(group, dtype=jnp.int32)
        member = row_ids[None, :] == group_ids[:, None]
        return jnp.max(jnp.where(member[:, :, None], part_top[None, :, :], very_low), axis=1)

    starts = jnp.arange(0, row_total_count, group, dtype=jnp.int32)
    block_top = lax.map(group_top, starts).reshape(row_total_count, part_top.shape[1])
    picked_top = pick_rows(block_top, row_ids, True)
    member_all = (row_ids[None, :] == jnp.arange(row_total_count, dtype=jnp.int32)[:, None]).astype(
        jnp.float32
    )
    block_total = jnp.dot(
        member_all,
        part_total * jnp.exp(part_top - picked_top),
        precision=lax.Precision.HIGHEST,
        preferred_element_type=jnp.float32,
    )
    return (block_top, block_total)


def on_device(src_points, tgt_points, log_src, log_tgt, tgt_potential, pattern):
    cell_count = src_points.shape[2]
    col_index = lax.axis_index("col")
    flat_targets = pattern.reshape(-1)
    all_points = lax.all_gather(tgt_points, "col", axis=0, tiled=True)
    all_potential = lax.all_gather(tgt_potential, "col", axis=0, tiled=True)
    slot_count = PAIR_MEAN
    chosen = col_index * slot_count + jnp.arange(slot_count, dtype=jnp.int32)
    slot_src = chosen // FANOUT
    slot_tgt = lax.dynamic_slice_in_dim(flat_targets, col_index * slot_count, slot_count, 0)
    in_use = jnp.ones((slot_count,), jnp.bool_)
    turn_count = slot_count // entry_batch
    slot_src_points = pick_rows(src_points, slot_src, False)
    slot_tgt_points = pick_rows(all_points, slot_tgt, False)
    slot_potential = pick_rows(all_potential, slot_tgt, True)
    point_shape = (turn_count, entry_batch) + src_points.shape[1:]
    batches = (
        slot_src_points.reshape(point_shape),
        slot_tgt_points.reshape(point_shape),
        in_use.reshape(turn_count, entry_batch),
    )

    def distances(src_block, tgt_block):
        products = jnp.einsum(
            "gdi,gdj->gij", src_block, tgt_block, preferred_element_type=jnp.float32
        )
        src_square = jnp.sum(jnp.square(src_block.astype(jnp.float32)), axis=1)
        tgt_square = jnp.sum(jnp.square(tgt_block.astype(jnp.float32)), axis=1)
        return (src_square[:, :, None] + tgt_square[:, None, :] - 2.0 * products) / DIM

    def row_terms(costs, potential_rows, used):
        scores = (potential_rows[:, None, :] - costs) / epsilon
        top_score = jnp.max(scores, axis=2)
        exp_total = jnp.sum(jnp.exp(scores - top_score[:, :, None]), axis=2)
        top_score = jnp.where(used[:, None], top_score, very_low)
        exp_total = jnp.where(used[:, None], exp_total, 0.0)
        return (top_score, exp_total)

    row_batches = batches + (slot_potential.reshape(turn_count, entry_batch, cell_count),)

    def row_fresh(state_in, members):
        return (state_in, row_terms(distances(members[0], members[1]), members[3], members[2]))

    row_out = lax.scan(row_fresh, None, row_batches)[1]
    row_top = row_out[0].reshape(slot_count, cell_count)
    row_total = row_out[1].reshape(slot_count, cell_count)
    own_count = slot_count // FANOUT
    own_start = col_index * own_count
    own_top = jnp.max(row_top.reshape(own_count, FANOUT, cell_count), axis=1)
    own_total = jnp.sum(
        (row_total * jnp.exp(row_top - jnp.repeat(own_top, FANOUT, axis=0))).reshape(
            own_count, FANOUT, cell_count
        ),
        axis=1,
    )
    own_log = lax.dynamic_slice_in_dim(log_src, own_start, own_count, 0)
    own_new = epsilon * own_log - epsilon * (own_top + jnp.log(own_total))
    src_new = lax.all_gather(own_new, "col", axis=0, tiled=True)
    slot_src_new = pick_rows(src_new, slot_src, True).reshape(turn_count, entry_batch, cell_count)

    def column_terms(costs, src_rows, used):
        weights = (src_rows[:, :, None] - costs) / epsilon
        top_score = jnp.max(weights, axis=1)
        exp_total = jnp.sum(jnp.exp(weights - top_score[:, None, :]), axis=1)
        top_score = jnp.where(used[:, None], top_score, very_low)
        exp_total = jnp.where(used[:, None], exp_total, 0.0)
        return (top_score, exp_total)

    def column_fresh(state_in, members):
        return (state_in, column_terms(distances(members[0], members[1]), members[3], members[2]))

    column_out = lax.scan(column_fresh, None, batches + (slot_src_new,))[1]
    column_top = column_out[0].reshape(slot_count, cell_count)
    column_total = column_out[1].reshape(slot_count, cell_count)
    tgt_rows = all_points.shape[0]
    target_top, target_total = collect_rows(tgt_rows, slot_tgt, column_top, column_total)
    sent_top, sent_total = (
        lax.all_to_all(target_top[:, None, :], "col", split_axis=0, concat_axis=1, tiled=True),
        lax.all_to_all(target_total[:, None, :], "col", split_axis=0, concat_axis=1, tiled=True),
    )
    local_top = jnp.max(sent_top, axis=1)
    local_total = jnp.sum(sent_total * jnp.exp(sent_top - local_top[:, None, :]), axis=1)
    final_top, final_total = joined((local_top, local_total), "row", merge_parts)
    tgt_new = epsilon * log_tgt - epsilon * (final_top + jnp.log(final_total))
    return (src_new, tgt_new)


def solution(mesh):
    placed = (
        P("row", None, None),
        P("col", None, None),
        P("row", None),
        P("col", None),
        P("col", None),
        P("row", None),
    )
    return jax.shard_map(
        on_device,
        mesh=mesh,
        in_specs=placed,
        out_specs=(P("row", None), P("col", None)),
        check_vma=False,
    )
```

profile of v0, /device:TPU:0, one launch (start us, length us, event | category | flops | bytes accessed | tf_op | source)
XLA Modules:
  0.0 134.5 jit_solution(16808524770713753963)
XLA Ops:
  7.2 0.7 all-gather.4.cloned.1.call-update
  7.9 0.8 copy.24
  8.8 3.0 %copy.32 = bf16[16,8,32,256]{3,1,2,0:T(8,128)(2,1)S(1)} copy(bf16[16,8,32,256]{3,2,1,0:T(8,128)(2,1)} %bitcast.132) | data formatting | bytes 4194304
  11.9 0.5 convolution_convert_fusion.1
  12.3 0.3 copy.25
  12.7 10.7 %all_gather.21 = f32[64,256]{1,0:T(8,128)S(1)} all-gather(f32[8,256]{1,0:T(8,128)S(1)} %copy-done), channel_id=1, replica_groups=mesh['row'=4,'col'=8] {'col'}, dimensions={0}, use_global_device_ids=true | all-gather | bytes 73728 | tf_op jit(solution)/shard_map/all_gather | solution.py:74
  23.6 12.4 %all-gather.4.cloned.1.call-done = bf16[64,32,256]{2,1,0:T(8,128)(2,1)} async-done(((bf16[8,32,256]{2,1,0:T(8,128)(2,1)}), bf16[64,32,256]{2,1,0:T(8,128)(2,1)}) %all-gather.4.cloned.1.call-update) | async-done | bytes 1048592 | tf_op jit(solution)/shard_map/all_gather | solution.py:73
  36.0 1.9 %copy.33 = bf16[8,8,32,256]{3,1,2,0:T(8,128)(2,1)S(1)} copy(bf16[8,8,32,256]{3,2,1,0:T(8,128)(2,1)} %bitcast.133) | data formatting | bytes 2097152
  37.9 0.5 convolution_convert_fusion
  38.4 0.3 copy.26
  38.7 14.9 %while.46 = (s32[]{:T(128)}, f32[8,8,256]{2,1,0:T(8,128)S(1)}, f32[8,8,256]{2,1,0:T(8,128)S(1)}, f32[8,8,256]{2,1,0:T(8,128)S(1)}, bf16[8,8,32,256]{3,2,1,0:T(8,...) while((s32[]{:T(128)}, f32[8,8,256]{2,1,0:T(8,128)S(1)}, f32[8,8,256]{2,1,0:T(8,128)S(1)}, ...), condition=%wide.region_5.6_spmd, body=%wide.region_0.5_spmd.sunk | while | flops 38658048 | bytes 4834397 | solution.py:112
  38.8 1.4 %fusion.34 = (f32[8,256]{1,0:T(8,128)S(1)}, f32[8,256,256]{1,2,0:T(8,128)S(1)}) fusion(bf16[8,8,32,256]{3,2,1,0:T(8,128)(2,1)S(1)} %get-tuple-element.407, s32[]{:T(128)} %get-tuple-element.395, bf16[8,8,32,256]{3,2,1,0:T(8,128)(2,1)S(1)} %get-tuple-element.406, f32[8,256]{1,0:T(8,128)S(1)} %get-tuple-element.362, ...), kind=kOutput, calls=%fused_computation.64.clone.1 | convolution fusion | flops 37222400 | bytes 2393088 | tf_op jit(solution)/shard_map/while/body/eval_jaxpr/gdi,gdj->gij/dot_general | solution.py:92
  40.2 0.3 exponential_reduce_fusion.4
  40.6 1.4 %fusion.34 = (f32[8,256]{1,0:T(8,128)S(1)}, f32[8,256,256]{1,2,0:T(8,128)S(1)}) fusion(bf16[8,8,32,256]{3,2,1,0:T(8,128)(2,1)S(1)} %get-tuple-element.407, s32[]{:T(128)} %get-tuple-element.395, bf16[8,8,32,256]{3,2,1,0:T(8,128)(2,1)S(1)} %get-tuple-element.406, f32[8,256]{1,0:T(8,128)S(1)} %get-tuple-element.362, ...), kind=kOutput, calls=%fused_computation.64.clone.1 | convolution fusion | flops 37222400 | bytes 2393088 | tf_op jit(solution)/shard_map/while/body/eval_jaxpr/gdi,gdj->gij/dot_general | solution.py:92
  42.1 0.3 exponential_reduce_fusion.4
  42.5 1.4 %fusion.34 = (f32[8,256]{1,0:T(8,128)S(1)}, f32[8,256,256]{1,2,0:T(8,128)S(1)}) fusion(bf16[8,8,32,256]{3,2,1,0:T(8,128)(2,1)S(1)} %get-tuple-element.407, s32[]{:T(128)} %get-tuple-element.395, bf16[8,8,32,256]{3,2,1,0:T(8,128)(2,1)S(1)} %get-tuple-element.406, f32[8,256]{1,0:T(8,128)S(1)} %get-tuple-element.362, ...), kind=kOutput, calls=%fused_computation.64.clone.1 | convolution fusion | flops 37222400 | bytes 2393088 | tf_op jit(solution)/shard_map/while/body/eval_jaxpr/gdi,gdj->gij/dot_general | solution.py:92
  43.9 0.3 exponential_reduce_fusion.4
  44.4 1.4 %fusion.34 = (f32[8,256]{1,0:T(8,128)S(1)}, f32[8,256,256]{1,2,0:T(8,128)S(1)}) fusion(bf16[8,8,32,256]{3,2,1,0:T(8,128)(2,1)S(1)} %get-tuple-element.407, s32[]{:T(128)} %get-tuple-element.395, bf16[8,8,32,256]{3,2,1,0:T(8,128)(2,1)S(1)} %get-tuple-element.406, f32[8,256]{1,0:T(8,128)S(1)} %get-tuple-element.362, ...), kind=kOutput, calls=%fused_computation.64.clone.1 | convolution fusion | flops 37222400 | bytes 2393088 | tf_op jit(solution)/shard_map/while/body/eval_jaxpr/gdi,gdj->gij/dot_general | solution.py:92
  45.8 0.3 exponential_reduce_fusion.4
  46.2 1.4 %fusion.34 = (f32[8,256]{1,0:T(8,128)S(1)}, f32[8,256,256]{1,2,0:T(8,128)S(1)}) fusion(bf16[8,8,32,256]{3,2,1,0:T(8,128)(2,1)S(1)} %get-tuple-element.407, s32[]{:T(128)} %get-tuple-element.395, bf16[8,8,32,256]{3,2,1,0:T(8,128)(2,1)S(1)} %get-tuple-element.406, f32[8,256]{1,0:T(8,128)S(1)} %get-tuple-element.362, ...), kind=kOutput, calls=%fused_computation.64.clone.1 | convolution fusion | flops 37222400 | bytes 2393088 | tf_op jit(solution)/shard_map/while/body/eval_jaxpr/gdi,gdj->gij/dot_general | solution.py:92
  47.7 0.3 exponential_reduce_fusion.4
  48.1 1.4 %fusion.34 = (f32[8,256]{1,0:T(8,128)S(1)}, f32[8,256,256]{1,2,0:T(8,128)S(1)}) fusion(bf16[8,8,32,256]{3,2,1,0:T(8,128)(2,1)S(1)} %get-tuple-element.407, s32[]{:T(128)} %get-tuple-element.395, bf16[8,8,32,256]{3,2,1,0:T(8,128)(2,1)S(1)} %get-tuple-element.406, f32[8,256]{1,0:T(8,128)S(1)} %get-tuple-element.362, ...), kind=kOutput, calls=%fused_computation.64.clone.1 | convolution fusion | flops 37222400 | bytes 2393088 | tf_op jit(solution)/shard_map/while/body/eval_jaxpr/gdi,gdj->gij/dot_general | solution.py:92
  49.5 0.3 exponential_reduce_fusion.4
  50.0 1.4 %fusion.34 = (f32[8,256]{1,0:T(8,128)S(1)}, f32[8,256,256]{1,2,0:T(8,128)S(1)}) fusion(bf16[8,8,32,256]{3,2,1,0:T(8,128)(2,1)S(1)} %get-tuple-element.407, s32[]{:T(128)} %get-tuple-element.395, bf16[8,8,32,256]{3,2,1,0:T(8,128)(2,1)S(1)} %get-tuple-element.406, f32[8,256]{1,0:T(8,128)S(1)} %get-tuple-element.362, ...), kind=kOutput, calls=%fused_computation.64.clone.1 | convolution fusion | flops 37222400 | bytes 2393088 | tf_op jit(solution)/shard_map/while/body/eval_jaxpr/gdi,gdj->gij/dot_general | solution.py:92
  51.4 0.3 exponential_reduce_fusion.4
  51.8 1.4 %fusion.34 = (f32[8,256]{1,0:T(8,128)S(1)}, f32[8,256,256]{1,2,0:T(8,128)S(1)}) fusion(bf16[8,8,32,256]{3,2,1,0:T(8,128)(2,1)S(1)} %get-tuple-element.407, s32[]{:T(128)} %get-tuple-element.395, bf16[8,8,32,256]{3,2,1,0:T(8,128)(2,1)S(1)} %get-tuple-element.406, f32[8,256]{1,0:T(8,128)S(1)} %get-tuple-element.362, ...), kind=kOutput, calls=%fused_computation.64.clone.1 | convolution fusion | flops 37222400 | bytes 2393088 | tf_op jit(solution)/shard_map/while/body/eval_jaxpr/gdi,gdj->gij/dot_general | solution.py:92
  53.3 0.3 exponential_reduce_fusion.4
  53.8 0.7 multiply_subtract_fusion
  54.5 9.2 %all_gather.23 = f32[128,256]{1,0:T(8,128)S(1)} all-gather(f32[16,256]{1,0:T(8,128)S(1)} %multiply_subtract_fusion), channel_id=1, replica_groups=mesh['row'=4,'col'=8] {'col'}, dimensions={0}, use_global_device_ids=true | all-gather | bytes 147456 | tf_op jit(solution)/shard_map/all_gather | solution.py:126
  63.9 14.9 %while.47 = (s32[]{:T(128)}, f32[8,8,256]{2,1,0:T(8,128)S(1)}, f32[8,8,256]{2,1,0:T(8,128)S(1)}, f32[8,8,256]{2,1,0:T(8,128)S(1)}, bf16[8,8,32,256]{3,2,1,0:T(8,...) while((s32[]{:T(128)}, f32[8,8,256]{2,1,0:T(8,128)S(1)}, f32[8,8,256]{2,1,0:T(8,128)S(1)}, ...), condition=%wide.region_13.14_spmd, body=%wide.region_8.13_spmd.sunk | while | flops 38658048 | bytes 4834397 | solution.py:140
  64.0 1.4 %fusion.35 = (f32[8,256]{1,0:T(8,128)S(1)}, f32[8,256,256]{2,1,0:T(8,128)S(1)}) fusion(bf16[8,8,32,256]{3,2,1,0:T(8,128)(2,1)S(1)} %get-tuple-element.428, s32[]{:T(128)} %get-tuple-element.416, bf16[8,8,32,256]{3,2,1,0:T(8,128)(2,1)S(1)} %get-tuple-element.427, f32[8,256]{1,0:T(8,128)S(1)} %get-tuple-element.372, ...), kind=kOutput, calls=%fused_computation.65.clone.1 | convolution fusion | flops 37222400 | bytes 2393088 | tf_op jit(solution)/shard_map/while/body/eval_jaxpr/gdi,gdj->gij/dot_general | solution.py:92
  65.5 0.3 exponential_reduce_fusion.5
  65.9 1.4 %fusion.35 = (f32[8,256]{1,0:T(8,128)S(1)}, f32[8,256,256]{2,1,0:T(8,128)S(1)}) fusion(bf16[8,8,32,256]{3,2,1,0:T(8,128)(2,1)S(1)} %get-tuple-element.428, s32[]{:T(128)} %get-tuple-element.416, bf16[8,8,32,256]{3,2,1,0:T(8,128)(2,1)S(1)} %get-tuple-element.427, f32[8,256]{1,0:T(8,128)S(1)} %get-tuple-element.372, ...), kind=kOutput, calls=%fused_computation.65.clone.1 | convolution fusion | flops 37222400 | bytes 2393088 | tf_op jit(solution)/shard_map/while/body/eval_jaxpr/gdi,gdj->gij/dot_general | solution.py:92
  67.3 0.3 exponential_reduce_fusion.5
  67.8 1.4 %fusion.35 = (f32[8,256]{1,0:T(8,128)S(1)}, f32[8,256,256]{2,1,0:T(8,128)S(1)}) fusion(bf16[8,8,32,256]{3,2,1,0:T(8,128)(2,1)S(1)} %get-tuple-element.428, s32[]{:T(128)} %get-tuple-element.416, bf16[8,8,32,256]{3,2,1,0:T(8,128)(2,1)S(1)} %get-tuple-element.427, f32[8,256]{1,0:T(8,128)S(1)} %get-tuple-element.372, ...), kind=kOutput, calls=%fused_computation.65.clone.1 | convolution fusion | flops 37222400 | bytes 2393088 | tf_op jit(solution)/shard_map/while/body/eval_jaxpr/gdi,gdj->gij/dot_general | solution.py:92
  69.2 0.3 exponential_reduce_fusion.5
  69.7 1.4 %fusion.35 = (f32[8,256]{1,0:T(8,128)S(1)}, f32[8,256,256]{2,1,0:T(8,128)S(1)}) fusion(bf16[8,8,32,256]{3,2,1,0:T(8,128)(2,1)S(1)} %get-tuple-element.428, s32[]{:T(128)} %get-tuple-element.416, bf16[8,8,32,256]{3,2,1,0:T(8,128)(2,1)S(1)} %get-tuple-element.427, f32[8,256]{1,0:T(8,128)S(1)} %get-tuple-element.372, ...), kind=kOutput, calls=%fused_computation.65.clone.1 | convolution fusion | flops 37222400 | bytes 2393088 | tf_op jit(solution)/shard_map/while/body/eval_jaxpr/gdi,gdj->gij/dot_general | solution.py:92
  71.1 0.3 exponential_reduce_fusion.5
  71.5 1.4 %fusion.35 = (f32[8,256]{1,0:T(8,128)S(1)}, f32[8,256,256]{2,1,0:T(8,128)S(1)}) fusion(bf16[8,8,32,256]{3,2,1,0:T(8,128)(2,1)S(1)} %get-tuple-element.428, s32[]{:T(128)} %get-tuple-element.416, bf16[8,8,32,256]{3,2,1,0:T(8,128)(2,1)S(1)} %get-tuple-element.427, f32[8,256]{1,0:T(8,128)S(1)} %get-tuple-element.372, ...), kind=kOutput, calls=%fused_computation.65.clone.1 | convolution fusion | flops 37222400 | bytes 2393088 | tf_op jit(solution)/shard_map/while/body/eval_jaxpr/gdi,gdj->gij/dot_general | solution.py:92
  72.9 0.3 exponential_reduce_fusion.5
  73.4 1.4 %fusion.35 = (f32[8,256]{1,0:T(8,128)S(1)}, f32[8,256,256]{2,1,0:T(8,128)S(1)}) fusion(bf16[8,8,32,256]{3,2,1,0:T(8,128)(2,1)S(1)} %get-tuple-element.428, s32[]{:T(128)} %get-tuple-element.416, bf16[8,8,32,256]{3,2,1,0:T(8,128)(2,1)S(1)} %get-tuple-element.427, f32[8,256]{1,0:T(8,128)S(1)} %get-tuple-element.372, ...), kind=kOutput, calls=%fused_computation.65.clone.1 | convolution fusion | flops 37222400 | bytes 2393088 | tf_op jit(solution)/shard_map/while/body/eval_jaxpr/gdi,gdj->gij/dot_general | solution.py:92
  74.8 0.3 exponential_reduce_fusion.5
  75.3 1.4 %fusion.35 = (f32[8,256]{1,0:T(8,128)S(1)}, f32[8,256,256]{2,1,0:T(8,128)S(1)}) fusion(bf16[8,8,32,256]{3,2,1,0:T(8,128)(2,1)S(1)} %get-tuple-element.428, s32[]{:T(128)} %get-tuple-element.416, bf16[8,8,32,256]{3,2,1,0:T(8,128)(2,1)S(1)} %get-tuple-element.427, f32[8,256]{1,0:T(8,128)S(1)} %get-tuple-element.372, ...), kind=kOutput, calls=%fused_computation.65.clone.1 | convolution fusion | flops 37222400 | bytes 2393088 | tf_op jit(solution)/shard_map/while/body/eval_jaxpr/gdi,gdj->gij/dot_general | solution.py:92
  76.7 0.3 exponential_reduce_fusion.5
  77.1 1.4 %fusion.35 = (f32[8,256]{1,0:T(8,128)S(1)}, f32[8,256,256]{2,1,0:T(8,128)S(1)}) fusion(bf16[8,8,32,256]{3,2,1,0:T(8,128)(2,1)S(1)} %get-tuple-element.428, s32[]{:T(128)} %get-tuple-element.416, bf16[8,8,32,256]{3,2,1,0:T(8,128)(2,1)S(1)} %get-tuple-element.427, f32[8,256]{1,0:T(8,128)S(1)} %get-tuple-element.372, ...), kind=kOutput, calls=%fused_computation.65.clone.1 | convolution fusion | flops 37222400 | bytes 2393088 | tf_op jit(solution)/shard_map/while/body/eval_jaxpr/gdi,gdj->gij/dot_general | solution.py:92
  78.5 0.3 exponential_reduce_fusion.5
  78.9 3.7 %while.48 = (s32[]{:T(128)}, f32[2,32,256]{2,1,0:T(8,128)S(1)}, s32[64]{0:T(128)S(1)}, s32[2]{0:T(128)S(1)}, f32[8,8,256]{2,1,0:T(8,128)S(1)}, /*index=5*/s32[]{:T(128)}) while((s32[]{:T(128)}, f32[2,32,256]{2,1,0:T(8,128)S(1)}, s32[64]{0:T(128)S(1)}, s32[2]{0:T(128)S(1)}, f32[8,8,256]{2,1,0:T(8,128)S(1)}, /*index=5*/s32[]{:T(128)}) %tuple.90), condition=%wide.region_16.17_spmd, body=%wide.region_14.16_spmd.sunk | while | flops 1042466 | bytes 168537 | solution.py:55
  78.9 0.6 dynamic_slice.95
  79.5 0.6 iota_add_fusion.2
  80.2 0.5 select_reduce_fusion.2
  80.8 0.6 dynamic_slice.95
  81.3 0.6 iota_add_fusion.2
  82.1 0.5 select_reduce_fusion.2
  82.6 0.7 broadcast_in_dim_reshape.4
  83.3 3.4 %all-to-all-start = ((f32[64,1,256]{2,1,0:T(1,128)}), f32[64,1,256]{2,1,0:T(1,128)S(1)}, u32[]{:S(2)}, u32[]{:S(2)}) async-start(f32[64,1,256]{2,1,0:T(1,128)} %broadcast_in_dim_reshape.4), calls=%async_computation | async-start | bytes 131072 | tf_op jit(solution)/shard_map/all_to_all | solution.py:146
  86.7 0.2 fusion.13
  87.1 0.7 copy.29
  87.8 3.8 %all-to-all-done = f32[64,1,256]{2,1,0:T(1,128)S(1)} async-done(((f32[64,1,256]{2,1,0:T(1,128)}), f32[64,1,256]{2,1,0:T(1,128)S(1)}, u32[]{:S(2)}, u32[]{:S(2)}) %all-to-all-start) | async-done | bytes 65568 | tf_op jit(solution)/shard_map/all_to_all | solution.py:146
  91.6 3.3 %all-to-all-start.1 = ((f32[64,1,256]{2,1,0:T(1,128)}), f32[64,1,256]{2,1,0:T(1,128)S(1)}, u32[]{:S(2)}, u32[]{:S(2)}) async-start(f32[64,1,256]{2,1,0:T(1,128)} %copy.29), calls=%async_computation.1 | async-start | bytes 131072 | tf_op jit(solution)/shard_map/all_to_all | solution.py:147
  95.0 4.9 %all-to-all-done.1 = f32[64,1,256]{2,1,0:T(1,128)S(1)} async-done(((f32[64,1,256]{2,1,0:T(1,128)}), f32[64,1,256]{2,1,0:T(1,128)S(1)}, u32[]{:S(2)}, u32[]{:S(2)}) %all-to-all-start.1) | async-done | bytes 65568 | tf_op jit(solution)/shard_map/all_to_all | solution.py:147
  100.0 13.2 %all-gather.1 = f32[32,256]{1,0:T(8,128)S(1)} all-gather(f32[8,256]{1,0:T(8,128)S(1)} %fusion.16), channel_id=3, replica_groups=mesh['row'=4,'col'=8] {'row'}, dimensions={0}, use_global_device_ids=true | all-gather | bytes 40960 | tf_op jit(solution)/shard_map/all_gather | solution.py:16
  113.1 13.1 %all-gather = f32[32,256]{1,0:T(8,128)S(1)} all-gather(f32[8,256]{1,0:T(8,128)S(1)} %reduce_max.50), channel_id=2, replica_groups=mesh['row'=4,'col'=8] {'row'}, dimensions={0}, use_global_device_ids=true | all-gather | bytes 40960 | tf_op jit(solution)/shard_map/all_gather | solution.py:16
  126.4 0.6 multiply_subtract_fusion.1
  127.0 0.7 copy.77
  (99 shorter events, 3.2 us)
Async XLA Ops:
  7.2 28.9 %all-gather.4.cloned.1.call-start = ((), (), s32[]{:S(2)}) async-start(), calls=%async_computation.2 | async-start | bytes 1179648 | tf_op jit(solution)/shard_map/all_gather | solution.py:73
  11.8 0.9 copy-start
  78.9 47.5 %copy-start.1 = (f32[8,256]{1,0:T(8,128)S(1)}, f32[8,256]{1,0:T(8,128)}, u32[]{:S(2)}) copy-start(f32[8,256]{1,0:T(8,128)} %param.17) | copy-start | bytes 24580
  83.3 8.3 %all-to-all-start = ((f32[64,1,256]{2,1,0:T(1,128)}), f32[64,1,256]{2,1,0:T(1,128)S(1)}, u32[]{:S(2)}, u32[]{:S(2)}) async-start(f32[64,1,256]{2,1,0:T(1,128)} %broadcast_in_dim_reshape.4), calls=%async_computation | async-start | bytes 131072 | tf_op jit(solution)/shard_map/all_to_all | solution.py:146
  91.6 8.3 %all-to-all-start.1 = ((f32[64,1,256]{2,1,0:T(1,128)}), f32[64,1,256]{2,1,0:T(1,128)S(1)}, u32[]{:S(2)}, u32[]{:S(2)}) async-start(f32[64,1,256]{2,1,0:T(1,128)} %copy.29), calls=%async_computation.1 | async-start | bytes 131072 | tf_op jit(solution)/shard_map/all_to_all | solution.py:147
Sparse Core Ops, SparseCore 0:
  9.9 26.1 all-gather.3
where the time goes:
time: 135 us
  blocking collectives  46.2 us (34%)
  matrix products  24.2 us (18%)
  waiting for transfers between devices  21.8 us (16%)
  between operations  14.3 us (11%)
  other arithmetic  10.1 us (7%)
  local copies, waits for them, and re-layouts  10.1 us (7%)
  starting transfers between devices  6.74 us (5%)
    all_gather x2, blocking collectives, joined(): pieces = jax.tree.map(lambda part: lax.all_gather(part, axis), value)  26.3 us
    dot_general x16, matrix products, distances(): jnp.einsum('gdi,gdj->gij', src_block, tgt_block, preferred_element_type=j...  22.4 us
    all_gather x1, waiting for transfers between devices, on_device(): all_points = lax.all_gather(tgt_points, 'col', axis=0, tiled=True)  12.4 us
    all_gather x1, blocking collectives, on_device(): all_potential = lax.all_gather(tgt_potential, 'col', axis=0, tiled=True)  10.7 us
    all_gather x1, blocking collectives, on_device(): src_new = lax.all_gather(own_new, 'col', axis=0, tiled=True)  9.15 us
    unnamed x8, local copies, waits for them, and re-layouts  6.32 us
    all_to_all x1, waiting for transfers between devices, on_device(): lax.all_to_all(target_total[:, None, :], 'col', split_axis=0, concat_axis...  4.89 us
    all_to_all x1, waiting for transfers between devices, on_device(): lax.all_to_all(target_top[:, None, :], 'col', split_axis=0, concat_axis=1...  3.85 us
  transfers between devices with their start and end apart: 3, of which 3 were waited for; matrix products, arithmetic and copies ran while one was open for 5% of the time, Pallas kernels for 0%

commit v1 on v0

--- a/solution.py
+++ b/solution.py
@@ -144,7 +144,15 @@
     target_top, target_total = collect_rows(tgt_rows, slot_tgt, column_top, column_total)
     sent_top, sent_total = (
         lax.all_to_all(target_top[:, None, :], "col", split_axis=0, concat_axis=1, tiled=True),
-        lax.all_to_all(target_total[:, None, :], "col", split_axis=0, concat_axis=1, tiled=True),
+        jnp.concatenate(
+            lax.all_to_all(
+                jnp.stack(jnp.split(target_total[:, None, :], lax.axis_size("col"), axis=0)),
+                "col",
+                0,
+                0,
+            ),
+            axis=1,
+        ),
     )
     local_top = jnp.max(sent_top, axis=1)
     local_total = jnp.sum(sent_total * jnp.exp(sent_top - local_top[:, None, :]), axis=1)

time: 135 us -> 140 us (1.037)
  local copies, waits for them, and re-layouts: 10.1 us -> 14.1 us
    unnamed x8 -> x15, local copies, waits for them, and re-layouts: 6.32 us -> 10.5 us
  transfers between devices with their start and end apart: 3 -> 3, of which waited for: 3 -> 3; matrix products, arithmetic and copies ran while one was open for 5% -> 4% of each run, Pallas kernels for 0% -> 0%
where the time goes in v1:
time: 140 us; the launch traced here: 139 us
  blocking collectives  46.2 us (33%)
  matrix products  24.2 us (17%)
  waiting for transfers between devices  22.3 us (16%)
  between operations  14.3 us (10%)
  local copies, waits for them, and re-layouts  14.1 us (10%)
  other arithmetic  10.1 us (7%)
  starting transfers between devices  6.74 us (5%)
    all_gather x2, blocking collectives, joined(): pieces = jax.tree.map(lambda part: lax.all_gather(part, axis), value)  26.3 us
    dot_general x16, matrix products, distances(): jnp.einsum('gdi,gdj->gij', src_block, tgt_block, preferred_element_type=j...  22.4 us
    all_gather x1, waiting for transfers between devices, on_device(): all_points = lax.all_gather(tgt_points, 'col', axis=0, tiled=True)  12.4 us
    all_gather x1, blocking collectives, on_device(): all_potential = lax.all_gather(tgt_potential, 'col', axis=0, tiled=True)  10.7 us
    unnamed x15, local copies, waits for them, and re-layouts  10.5 us
    all_gather x1, blocking collectives, on_device(): src_new = lax.all_gather(own_new, 'col', axis=0, tiled=True)  9.15 us
    all_to_all x1, waiting for transfers between devices, on_device(): lax.all_to_all(jnp.stack(jnp.split(target_total[:, None, :], lax.axis_siz...  4.93 us
    all_to_all x1, waiting for transfers between devices, on_device(): lax.all_to_all(target_top[:, None, :], 'col', split_axis=0, concat_axis=1...  4.35 us
  transfers between devices with their start and end apart: 3, of which 3 were waited for; matrix products, arithmetic and copies ran while one was open for 4% of the time, Pallas kernels for 0%

profile of v1, /device:TPU:0, one launch (start us, length us, event | category | flops | bytes accessed | tf_op | source)
XLA Modules:
  0.0 139.1 jit_solution(10275742157607524991)
XLA Ops:
  7.2 0.7 all-gather.4.cloned.1.call-update
  7.9 0.8 copy.22
  8.8 3.0 %copy.28 = bf16[16,8,32,256]{3,1,2,0:T(8,128)(2,1)S(1)} copy(bf16[16,8,32,256]{3,2,1,0:T(8,128)(2,1)} %bitcast.164) | data formatting | bytes 4194304
  11.9 0.5 convolution_convert_fusion.1
  12.7 10.7 %all_gather.21 = f32[64,256]{1,0:T(8,128)S(1)} all-gather(f32[8,256]{1,0:T(8,128)S(1)} %copy-done), channel_id=1, replica_groups=mesh['row'=4,'col'=8] {'col'}, dimensions={0}, use_global_device_ids=true | all-gather | bytes 73728 | tf_op jit(solution)/shard_map/all_gather | solution.py:74
  23.6 12.4 %all-gather.4.cloned.1.call-done = bf16[64,32,256]{2,1,0:T(8,128)(2,1)} async-done(((bf16[8,32,256]{2,1,0:T(8,128)(2,1)}), bf16[64,32,256]{2,1,0:T(8,128)(2,1)}) %all-gather.4.cloned.1.call-update) | async-done | bytes 1048592 | tf_op jit(solution)/shard_map/all_gather | solution.py:73
  36.0 1.9 %copy.29 = bf16[8,8,32,256]{3,1,2,0:T(8,128)(2,1)S(1)} copy(bf16[8,8,32,256]{3,2,1,0:T(8,128)(2,1)} %bitcast.165) | data formatting | bytes 2097152
  37.9 0.5 convolution_convert_fusion
  38.7 14.9 %while.46 = (s32[]{:T(128)}, f32[8,8,256]{2,1,0:T(8,128)S(1)}, f32[8,8,256]{2,1,0:T(8,128)S(1)}, f32[8,8,256]{2,1,0:T(8,128)S(1)}, bf16[8,8,32,256]{3,2,1,0:T(8,...) while((s32[]{:T(128)}, f32[8,8,256]{2,1,0:T(8,128)S(1)}, f32[8,8,256]{2,1,0:T(8,128)S(1)}, ...), condition=%wide.region_5.6_spmd, body=%wide.region_0.5_spmd.sunk | while | flops 38658048 | bytes 4834397 | solution.py:112
  38.8 1.4 %fusion.35 = (f32[8,256]{1,0:T(8,128)S(1)}, f32[8,256,256]{1,2,0:T(8,128)S(1)}) fusion(bf16[8,8,32,256]{3,2,1,0:T(8,128)(2,1)S(1)} %get-tuple-element.407, s32[]{:T(128)} %get-tuple-element.395, bf16[8,8,32,256]{3,2,1,0:T(8,128)(2,1)S(1)} %get-tuple-element.406, f32[8,256]{1,0:T(8,128)S(1)} %get-tuple-element.362, ...), kind=kOutput, calls=%fused_computation.81.clone.1 | convolution fusion | flops 37222400 | bytes 2393088 | tf_op jit(solution)/shard_map/while/body/eval_jaxpr/gdi,gdj->gij/dot_general | solution.py:92
  40.2 0.3 exponential_reduce_fusion.4
  40.6 1.4 %fusion.35 = (f32[8,256]{1,0:T(8,128)S(1)}, f32[8,256,256]{1,2,0:T(8,128)S(1)}) fusion(bf16[8,8,32,256]{3,2,1,0:T(8,128)(2,1)S(1)} %get-tuple-element.407, s32[]{:T(128)} %get-tuple-element.395, bf16[8,8,32,256]{3,2,1,0:T(8,128)(2,1)S(1)} %get-tuple-element.406, f32[8,256]{1,0:T(8,128)S(1)} %get-tuple-element.362, ...), kind=kOutput, calls=%fused_computation.81.clone.1 | convolution fusion | flops 37222400 | bytes 2393088 | tf_op jit(solution)/shard_map/while/body/eval_jaxpr/gdi,gdj->gij/dot_general | solution.py:92
  42.1 0.3 exponential_reduce_fusion.4
  42.5 1.4 %fusion.35 = (f32[8,256]{1,0:T(8,128)S(1)}, f32[8,256,256]{1,2,0:T(8,128)S(1)}) fusion(bf16[8,8,32,256]{3,2,1,0:T(8,128)(2,1)S(1)} %get-tuple-element.407, s32[]{:T(128)} %get-tuple-element.395, bf16[8,8,32,256]{3,2,1,0:T(8,128)(2,1)S(1)} %get-tuple-element.406, f32[8,256]{1,0:T(8,128)S(1)} %get-tuple-element.362, ...), kind=kOutput, calls=%fused_computation.81.clone.1 | convolution fusion | flops 37222400 | bytes 2393088 | tf_op jit(solution)/shard_map/while/body/eval_jaxpr/gdi,gdj->gij/dot_general | solution.py:92
  43.9 0.3 exponential_reduce_fusion.4
  44.4 1.4 %fusion.35 = (f32[8,256]{1,0:T(8,128)S(1)}, f32[8,256,256]{1,2,0:T(8,128)S(1)}) fusion(bf16[8,8,32,256]{3,2,1,0:T(8,128)(2,1)S(1)} %get-tuple-element.407, s32[]{:T(128)} %get-tuple-element.395, bf16[8,8,32,256]{3,2,1,0:T(8,128)(2,1)S(1)} %get-tuple-element.406, f32[8,256]{1,0:T(8,128)S(1)} %get-tuple-element.362, ...), kind=kOutput, calls=%fused_computation.81.clone.1 | convolution fusion | flops 37222400 | bytes 2393088 | tf_op jit(solution)/shard_map/while/body/eval_jaxpr/gdi,gdj->gij/dot_general | solution.py:92
  45.8 0.3 exponential_reduce_fusion.4
  46.2 1.4 %fusion.35 = (f32[8,256]{1,0:T(8,128)S(1)}, f32[8,256,256]{1,2,0:T(8,128)S(1)}) fusion(bf16[8,8,32,256]{3,2,1,0:T(8,128)(2,1)S(1)} %get-tuple-element.407, s32[]{:T(128)} %get-tuple-element.395, bf16[8,8,32,256]{3,2,1,0:T(8,128)(2,1)S(1)} %get-tuple-element.406, f32[8,256]{1,0:T(8,128)S(1)} %get-tuple-element.362, ...), kind=kOutput, calls=%fused_computation.81.clone.1 | convolution fusion | flops 37222400 | bytes 2393088 | tf_op jit(solution)/shard_map/while/body/eval_jaxpr/gdi,gdj->gij/dot_general | solution.py:92
  47.7 0.3 exponential_reduce_fusion.4
  48.1 1.4 %fusion.35 = (f32[8,256]{1,0:T(8,128)S(1)}, f32[8,256,256]{1,2,0:T(8,128)S(1)}) fusion(bf16[8,8,32,256]{3,2,1,0:T(8,128)(2,1)S(1)} %get-tuple-element.407, s32[]{:T(128)} %get-tuple-element.395, bf16[8,8,32,256]{3,2,1,0:T(8,128)(2,1)S(1)} %get-tuple-element.406, f32[8,256]{1,0:T(8,128)S(1)} %get-tuple-element.362, ...), kind=kOutput, calls=%fused_computation.81.clone.1 | convolution fusion | flops 37222400 | bytes 2393088 | tf_op jit(solution)/shard_map/while/body/eval_jaxpr/gdi,gdj->gij/dot_general | solution.py:92
  49.5 0.3 exponential_reduce_fusion.4
  50.0 1.4 %fusion.35 = (f32[8,256]{1,0:T(8,128)S(1)}, f32[8,256,256]{1,2,0:T(8,128)S(1)}) fusion(bf16[8,8,32,256]{3,2,1,0:T(8,128)(2,1)S(1)} %get-tuple-element.407, s32[]{:T(128)} %get-tuple-element.395, bf16[8,8,32,256]{3,2,1,0:T(8,128)(2,1)S(1)} %get-tuple-element.406, f32[8,256]{1,0:T(8,128)S(1)} %get-tuple-element.362, ...), kind=kOutput, calls=%fused_computation.81.clone.1 | convolution fusion | flops 37222400 | bytes 2393088 | tf_op jit(solution)/shard_map/while/body/eval_jaxpr/gdi,gdj->gij/dot_general | solution.py:92
  51.4 0.3 exponential_reduce_fusion.4
  51.8 1.4 %fusion.35 = (f32[8,256]{1,0:T(8,128)S(1)}, f32[8,256,256]{1,2,0:T(8,128)S(1)}) fusion(bf16[8,8,32,256]{3,2,1,0:T(8,128)(2,1)S(1)} %get-tuple-element.407, s32[]{:T(128)} %get-tuple-element.395, bf16[8,8,32,256]{3,2,1,0:T(8,128)(2,1)S(1)} %get-tuple-element.406, f32[8,256]{1,0:T(8,128)S(1)} %get-tuple-element.362, ...), kind=kOutput, calls=%fused_computation.81.clone.1 | convolution fusion | flops 37222400 | bytes 2393088 | tf_op jit(solution)/shard_map/while/body/eval_jaxpr/gdi,gdj->gij/dot_general | solution.py:92
  53.8 0.7 multiply_subtract_fusion
  54.5 9.2 %all_gather.23 = f32[128,256]{1,0:T(8,128)S(1)} all-gather(f32[16,256]{1,0:T(8,128)S(1)} %multiply_subtract_fusion), channel_id=1, replica_groups=mesh['row'=4,'col'=8] {'col'}, dimensions={0}, use_global_device_ids=true | all-gather | bytes 147456 | tf_op jit(solution)/shard_map/all_gather | solution.py:126
  63.9 14.9 %while.47 = (s32[]{:T(128)}, f32[8,8,256]{2,1,0:T(8,128)S(1)}, f32[8,8,256]{2,1,0:T(8,128)S(1)}, f32[8,8,256]{2,1,0:T(8,128)S(1)}, bf16[8,8,32,256]{3,2,1,0:T(8,...) while((s32[]{:T(128)}, f32[8,8,256]{2,1,0:T(8,128)S(1)}, f32[8,8,256]{2,1,0:T(8,128)S(1)}, ...), condition=%wide.region_13.14_spmd, body=%wide.region_8.13_spmd.sunk | while | flops 38658048 | bytes 4834397 | solution.py:140
  64.0 1.4 %fusion.36 = (f32[8,256]{1,0:T(8,128)S(1)}, f32[8,256,256]{2,1,0:T(8,128)S(1)}) fusion(bf16[8,8,32,256]{3,2,1,0:T(8,128)(2,1)S(1)} %get-tuple-element.428, s32[]{:T(128)} %get-tuple-element.416, bf16[8,8,32,256]{3,2,1,0:T(8,128)(2,1)S(1)} %get-tuple-element.427, f32[8,256]{1,0:T(8,128)S(1)} %get-tuple-element.372, ...), kind=kOutput, calls=%fused_computation.82.clone.1 | convolution fusion | flops 37222400 | bytes 2393088 | tf_op jit(solution)/shard_map/while/body/eval_jaxpr/gdi,gdj->gij/dot_general | solution.py:92
  65.5 0.3 exponential_reduce_fusion.5
  65.9 1.4 %fusion.36 = (f32[8,256]{1,0:T(8,128)S(1)}, f32[8,256,256]{2,1,0:T(8,128)S(1)}) fusion(bf16[8,8,32,256]{3,2,1,0:T(8,128)(2,1)S(1)} %get-tuple-element.428, s32[]{:T(128)} %get-tuple-element.416, bf16[8,8,32,256]{3,2,1,0:T(8,128)(2,1)S(1)} %get-tuple-element.427, f32[8,256]{1,0:T(8,128)S(1)} %get-tuple-element.372, ...), kind=kOutput, calls=%fused_computation.82.clone.1 | convolution fusion | flops 37222400 | bytes 2393088 | tf_op jit(solution)/shard_map/while/body/eval_jaxpr/gdi,gdj->gij/dot_general | solution.py:92
  67.8 1.4 %fusion.36 = (f32[8,256]{1,0:T(8,128)S(1)}, f32[8,256,256]{2,1,0:T(8,128)S(1)}) fusion(bf16[8,8,32,256]{3,2,1,0:T(8,128)(2,1)S(1)} %get-tuple-element.428, s32[]{:T(128)} %get-tuple-element.416, bf16[8,8,32,256]{3,2,1,0:T(8,128)(2,1)S(1)} %get-tuple-element.427, f32[8,256]{1,0:T(8,128)S(1)} %get-tuple-element.372, ...), kind=kOutput, calls=%fused_computation.82.clone.1 | convolution fusion | flops 37222400 | bytes 2393088 | tf_op jit(solution)/shard_map/while/body/eval_jaxpr/gdi,gdj->gij/dot_general | solution.py:92
  69.2 0.3 exponential_reduce_fusion.5
  69.7 1.4 %fusion.36 = (f32[8,256]{1,0:T(8,128)S(1)}, f32[8,256,256]{2,1,0:T(8,128)S(1)}) fusion(bf16[8,8,32,256]{3,2,1,0:T(8,128)(2,1)S(1)} %get-tuple-element.428, s32[]{:T(128)} %get-tuple-element.416, bf16[8,8,32,256]{3,2,1,0:T(8,128)(2,1)S(1)} %get-tuple-element.427, f32[8,256]{1,0:T(8,128)S(1)} %get-tuple-element.372, ...), kind=kOutput, calls=%fused_computation.82.clone.1 | convolution fusion | flops 37222400 | bytes 2393088 | tf_op jit(solution)/shard_map/while/body/eval_jaxpr/gdi,gdj->gij/dot_general | solution.py:92
  71.1 0.3 exponential_reduce_fusion.5
  71.5 1.4 %fusion.36 = (f32[8,256]{1,0:T(8,128)S(1)}, f32[8,256,256]{2,1,0:T(8,128)S(1)}) fusion(bf16[8,8,32,256]{3,2,1,0:T(8,128)(2,1)S(1)} %get-tuple-element.428, s32[]{:T(128)} %get-tuple-element.416, bf16[8,8,32,256]{3,2,1,0:T(8,128)(2,1)S(1)} %get-tuple-element.427, f32[8,256]{1,0:T(8,128)S(1)} %get-tuple-element.372, ...), kind=kOutput, calls=%fused_computation.82.clone.1 | convolution fusion | flops 37222400 | bytes 2393088 | tf_op jit(solution)/shard_map/while/body/eval_jaxpr/gdi,gdj->gij/dot_general | solution.py:92
  73.4 1.4 %fusion.36 = (f32[8,256]{1,0:T(8,128)S(1)}, f32[8,256,256]{2,1,0:T(8,128)S(1)}) fusion(bf16[8,8,32,256]{3,2,1,0:T(8,128)(2,1)S(1)} %get-tuple-element.428, s32[]{:T(128)} %get-tuple-element.416, bf16[8,8,32,256]{3,2,1,0:T(8,128)(2,1)S(1)} %get-tuple-element.427, f32[8,256]{1,0:T(8,128)S(1)} %get-tuple-element.372, ...), kind=kOutput, calls=%fused_computation.82.clone.1 | convolution fusion | flops 37222400 | bytes 2393088 | tf_op jit(solution)/shard_map/while/body/eval_jaxpr/gdi,gdj->gij/dot_general | solution.py:92
  74.8 0.3 exponential_reduce_fusion.5
  75.3 1.4 %fusion.36 = (f32[8,256]{1,0:T(8,128)S(1)}, f32[8,256,256]{2,1,0:T(8,128)S(1)}) fusion(bf16[8,8,32,256]{3,2,1,0:T(8,128)(2,1)S(1)} %get-tuple-element.428, s32[]{:T(128)} %get-tuple-element.416, bf16[8,8,32,256]{3,2,1,0:T(8,128)(2,1)S(1)} %get-tuple-element.427, f32[8,256]{1,0:T(8,128)S(1)} %get-tuple-element.372, ...), kind=kOutput, calls=%fused_computation.82.clone.1 | convolution fusion | flops 37222400 | bytes 2393088 | tf_op jit(solution)/shard_map/while/body/eval_jaxpr/gdi,gdj->gij/dot_general | solution.py:92
  76.7 0.3 exponential_reduce_fusion.5
  77.1 1.4 %fusion.36 = (f32[8,256]{1,0:T(8,128)S(1)}, f32[8,256,256]{2,1,0:T(8,128)S(1)}) fusion(bf16[8,8,32,256]{3,2,1,0:T(8,128)(2,1)S(1)} %get-tuple-element.428, s32[]{:T(128)} %get-tuple-element.416, bf16[8,8,32,256]{3,2,1,0:T(8,128)(2,1)S(1)} %get-tuple-element.427, f32[8,256]{1,0:T(8,128)S(1)} %get-tuple-element.372, ...), kind=kOutput, calls=%fused_computation.82.clone.1 | convolution fusion | flops 37222400 | bytes 2393088 | tf_op jit(solution)/shard_map/while/body/eval_jaxpr/gdi,gdj->gij/dot_general | solution.py:92
  78.9 3.7 %while.48 = (s32[]{:T(128)}, f32[2,32,256]{2,1,0:T(8,128)S(1)}, s32[64]{0:T(128)S(1)}, s32[2]{0:T(128)S(1)}, f32[8,8,256]{2,1,0:T(8,128)S(1)}, /*index=5*/s32[]{:T(128)}) while((s32[]{:T(128)}, f32[2,32,256]{2,1,0:T(8,128)S(1)}, s32[64]{0:T(128)S(1)}, s32[2]{0:T(128)S(1)}, f32[8,8,256]{2,1,0:T(8,128)S(1)}, /*index=5*/s32[]{:T(128)}) %tuple.90), condition=%wide.region_16.17_spmd, body=%wide.region_14.16_spmd.sunk | while | flops 1042466 | bytes 168537 | solution.py:55
  78.9 0.6 dynamic_slice.95
  79.5 0.6 iota_add_fusion.2
  80.2 0.5 select_reduce_fusion.2
  80.8 0.6 dynamic_slice.95
  81.3 0.6 iota_add_fusion.2
  82.1 0.5 select_reduce_fusion.2
  82.6 0.7 broadcast_in_dim_reshape.4
  83.7 0.6 constant_dynamic-update-slice_fusion.7
  84.3 0.6 constant_dynamic-update-slice_fusion.6
  84.9 0.6 constant_dynamic-update-slice_fusion.5
  85.5 0.6 constant_dynamic-update-slice_fusion.4
  86.1 0.6 constant_dynamic-update-slice_fusion.3
  86.7 0.6 constant_dynamic-update-slice_fusion.2
  87.3 0.6 constant_dynamic-update-slice_fusion.1
  87.9 3.4 %all-to-all-start = ((f32[64,1,256]{2,1,0:T(1,128)}), f32[64,1,256]{2,1,0:T(1,128)S(1)}, u32[]{:S(2)}, u32[]{:S(2)}) async-start(f32[64,1,256]{2,1,0:T(1,128)} %broadcast_in_dim_reshape.4), calls=%async_computation | async-start | bytes 131072 | tf_op jit(solution)/shard_map/all_to_all | solution.py:146
  91.2 0.6 constant_dynamic-update-slice_fusion
  91.8 4.3 %all-to-all-done = f32[64,1,256]{2,1,0:T(1,128)S(1)} async-done(((f32[64,1,256]{2,1,0:T(1,128)}), f32[64,1,256]{2,1,0:T(1,128)S(1)}, u32[]{:S(2)}, u32[]{:S(2)}) %all-to-all-start) | async-done | bytes 65568 | tf_op jit(solution)/shard_map/all_to_all | solution.py:146
  96.2 3.3 %all-to-all-start.1 = ((f32[8,8,1,256]{3,1,2,0:T(8,128)}), f32[8,8,1,256]{3,1,2,0:T(8,128)S(1)}, u32[]{:S(2)}, u32[]{:S(2)}) async-start(f32[8,8,1,256]{3,1,2,0:T(8,128)} %constant_dynamic-update-slice_fusion), calls=%async_computation.1 | async-start | bytes 131072 | tf_op jit(solution)/shard_map/all_to_all | solution.py:148
  99.6 4.9 %all-to-all-done.1 = f32[8,8,1,256]{3,1,2,0:T(8,128)S(1)} async-done(((f32[8,8,1,256]{3,1,2,0:T(8,128)}), f32[8,8,1,256]{3,1,2,0:T(8,128)S(1)}, u32[]{:S(2)}, u32[]{:S(2)}) %all-to-all-start.1) | async-done | bytes 65568 | tf_op jit(solution)/shard_map/all_to_all | solution.py:148
  104.5 13.2 %all-gather.1 = f32[32,256]{1,0:T(8,128)S(1)} all-gather(f32[8,256]{1,0:T(8,128)S(1)} %fusion.16), channel_id=3, replica_groups=mesh['row'=4,'col'=8] {'row'}, dimensions={0}, use_global_device_ids=true | all-gather | bytes 40960 | tf_op jit(solution)/shard_map/all_gather | solution.py:16
  117.7 13.1 %all-gather = f32[32,256]{1,0:T(8,128)S(1)} all-gather(f32[8,256]{1,0:T(8,128)S(1)} %bitcast_reduce_fusion), channel_id=2, replica_groups=mesh['row'=4,'col'=8] {'row'}, dimensions={0}, use_global_device_ids=true | all-gather | bytes 40960 | tf_op jit(solution)/shard_map/all_gather | solution.py:16
  131.0 0.6 multiply_subtract_fusion.1
  131.6 0.7 copy.80
  (106 shorter events, 5.1 us)
Async XLA Ops:
  7.2 28.9 %all-gather.4.cloned.1.call-start = ((), (), s32[]{:S(2)}) async-start(), calls=%async_computation.2 | async-start | bytes 1179648 | tf_op jit(solution)/shard_map/all_gather | solution.py:73
  11.8 0.9 copy-start
  78.9 52.1 %copy-start.1 = (f32[8,256]{1,0:T(8,128)S(1)}, f32[8,256]{1,0:T(8,128)}, u32[]{:S(2)}) copy-start(f32[8,256]{1,0:T(8,128)} %param.17) | copy-start | bytes 24580
  87.9 8.3 %all-to-all-start = ((f32[64,1,256]{2,1,0:T(1,128)}), f32[64,1,256]{2,1,0:T(1,128)S(1)}, u32[]{:S(2)}, u32[]{:S(2)}) async-start(f32[64,1,256]{2,1,0:T(1,128)} %broadcast_in_dim_reshape.4), calls=%async_computation | async-start | bytes 131072 | tf_op jit(solution)/shard_map/all_to_all | solution.py:146
  96.2 8.3 %all-to-all-start.1 = ((f32[8,8,1,256]{3,1,2,0:T(8,128)}), f32[8,8,1,256]{3,1,2,0:T(8,128)S(1)}, u32[]{:S(2)}, u32[]{:S(2)}) async-start(f32[8,8,1,256]{3,1,2,0:T(8,128)} %constant_dynamic-update-slice_fusion), calls=%async_computation.1 | async-start | bytes 131072 | tf_op jit(solution)/shard_map/all_to_all | solution.py:148
Sparse Core Ops, SparseCore 0:
  9.9 26.1 all-gather.3
